TPU v7x, 32 devices: a whole 2x2x4 slice. The times are simulated.
32 devices in a mesh: mp: 4 (over z), dp: 4 (over x, core), tensor: 2 (over y).
Axes of the slice: x: 2, y: 2, z: 4, core: 2. Of those that a mesh axis runs over, the one named last changes fastest.
Arguments:
- tokens: bfloat16 [1024, 8192], P(('mp', 'tensor'), 'dp'), may hold values from -64 to 64
- norm_gain: float32 [2, 8192], replicated, may hold values from 0.5 to 1.5
- gate_weight: bfloat16 [2, 8192, 14336], P(None, 'dp', ('mp', 'tensor')), may hold values from -0.0625 to 0.0625
- up_weight: bfloat16 [2, 8192, 14336], P(None, 'dp', ('mp', 'tensor')), may hold values from -0.0625 to 0.0625
- down_weight: bfloat16 [2, 14336, 8192], P(None, 'mp', 'tensor'), may hold values from -0.046875 to 0.046875
- sketch: bfloat16 [8192, 512], P('tensor'), may hold values from -6 to 6
Outputs:
- final_basis: float32 [8192, 512], P('tensor', ('mp', 'dp'))
- projected: float32 [8192, 512], P('tensor', ('mp', 'dp'))
All inputs are finite; a program needn't handle non-finite values.
Results may differ from a plain program's by a relative error of at most 0.04.
Values may be sent and summed in bfloat16 or wider, within the bound.
No kernel may reach another device: no remote copies, remote signals or barrier semaphores. Data moves between devices by JAX's collectives and lax.ppermute only.
A program may use at most 192 MiB of HBM per device.

v0:
```python
import jax
import jax.numpy as jnp
from jax import lax
from jax.sharding import PartitionSpec as P

D = 8192


EPSILON = 1e-05
HIGHEST = lax.Precision.HIGHEST


def orthonormal_from(gram_total, matrix):
    lower_factor = jnp.linalg.cholesky(gram_total)
    return lax.linalg.triangular_solve(
        lower_factor, matrix, left_side=False, lower=True, transpose_a=True
    )


def gram_of(matrix):
    return lax.dot_general(matrix, matrix, (((0,), (0,)), ((), ())), precision=HIGHEST) / D


def orthonormal(partial_value):
    summed = lax.psum(partial_value, ("mp", "dp"))
    gram_total = lax.psum(gram_of(summed), "tensor")
    return orthonormal_from(gram_total, summed)


def sketch_product(left_acts, right_acts, matrix, tokens_all):
    inner_sums = lax.psum(jnp.dot(right_acts, matrix, precision=HIGHEST), "tensor")
    product = lax.dot_general(left_acts, inner_sums, (((0,), (0,)), ((), ())), precision=HIGHEST)
    return product / tokens_all


def project_block(block_normed, gate_weight, up_weight):
    gate_part = jnp.einsum(
        "crd,cdh->rch", block_normed, gate_weight, preferred_element_type=jnp.float32
    )
    up_part = jnp.einsum(
        "crd,cdh->rch", block_normed, up_weight, preferred_element_type=jnp.float32
    )
    return jnp.stack((gate_part, up_part), axis=2)


def on_device(tokens, norm_gain, gate_weight, up_weight, down_weight, sketch):
    token_groups = lax.axis_size(("mp", "tensor"))
    tokens_all = tokens.shape[0] * token_groups
    feature_count = tokens.shape[1]
    offset = lax.axis_index("dp") * feature_count
    local_gain = lax.dynamic_slice_in_dim(norm_gain, offset, feature_count, 1)
    local_values = tokens.astype(jnp.float32)
    local_total = lax.psum(jnp.sum(local_values * local_values, axis=1), "dp")
    local_root = lax.rsqrt(local_total / D + EPSILON)
    root_all = lax.all_gather(local_root, ("mp", "tensor"), axis=0, tiled=True)
    piece_values = lax.all_gather(tokens, ("mp", "tensor"), axis=0, tiled=True).astype(jnp.float32)
    piece_normed = (
        piece_values[None, :, :] * root_all[None, :, None] * local_gain[:, None, :]
    ).astype(jnp.bfloat16)
    all_terms = project_block(piece_normed, gate_weight, up_weight)
    summed = lax.psum_scatter(
        all_terms.astype(jnp.bfloat16), "dp", scatter_dimension=0, tiled=True
    ).astype(jnp.float32)
    hidden = (jax.nn.silu(summed[:, :, 0]) * summed[:, :, 1]).astype(jnp.bfloat16)
    partial_out = jnp.einsum(
        "rch,chd->rcd",
        lax.all_gather(hidden, "tensor", axis=2, tiled=True),
        down_weight,
        preferred_element_type=jnp.float32,
    )
    layer_out = lax.psum_scatter(partial_out, "mp", scatter_dimension=0, tiled=True)
    base_acts = layer_out[:, 0, :]
    inst_acts = layer_out[:, 1, :]
    first_basis = orthonormal(
        sketch_product(base_acts, inst_acts, sketch.astype(jnp.float32), tokens_all)
    )
    second_basis = orthonormal(sketch_product(inst_acts, base_acts, first_basis, tokens_all))
    final_basis = orthonormal(sketch_product(base_acts, inst_acts, second_basis, tokens_all))
    core_part = sketch_product(inst_acts, base_acts, final_basis, tokens_all)
    projected = lax.psum_scatter(core_part, ("mp", "dp"), scatter_dimension=1, tiled=True)
    share_width = final_basis.shape[1] // lax.axis_size(("mp", "dp"))
    basis_share = lax.dynamic_slice_in_dim(
        final_basis, lax.axis_index(("mp", "dp")) * share_width, share_width, 1
    )
    return (basis_share, projected)


def solution(mesh):
    return jax.shard_map(
        on_device,
        mesh=mesh,
        in_specs=(
            P(("mp", "tensor"), "dp"),
            P(),
            P(None, "dp", ("mp", "tensor")),
            P(None, "dp", ("mp", "tensor")),
            P(None, "mp", "tensor"),
            P("tensor", None),
        ),
        out_specs=(P("tensor", ("mp", "dp")), P("tensor", ("mp", "dp"))),
        check_vma=False,
    )
```

profile of v0, /device:TPU:0, one launch (start us, length us, event | category | flops | bytes accessed | tf_op | source)
XLA Modules:
  0.0 1975.6 jit_solution(10811620839492787215)
XLA Ops:
  17.6 21.4 %all-gather = f32[8,1,128]{2,1,0:T(1,128)S(1)} all-gather(f32[1,1,128]{2,1,0:T(1,128)S(1)} %rsqrt_bitcast_fusion), channel_id=1, replica_groups=mesh['mp'=4,'dp'=4,'tensor'=2] {'mp','tensor'}, dimensions={0}, use_global_device_ids=true | all-gather | bytes 4608 | tf_op jit(solution)/shard_map/all_gather | solution.py:55
  38.9 46.8 %all-gather.4.cloned.1.call-done = bf16[1024,2048]{1,0:T(8,128)(2,1)} async-done(((bf16[128,2048]{1,0:T(8,128)(2,1)}), bf16[1024,2048]{1,0:T(8,128)(2,1)}) %all-gather.4.cloned.1.call-update) | async-done | bytes 4194320 | tf_op jit(solution)/shard_map/all_gather | solution.py:56
  88.5 18.7 convert_bitcast_fusion
  107.2 20.5 %convert_bitcast_fusion.1 = bf16[1024,2,1,1792]{3,0,1,2:T(8,128)(2,1)} fusion(bf16[2,2048,1792]{2,1,0:T(8,128)(2,1)} %param.11, f32[2,2048]{1,0:T(2,128)S(1)} %constant_dynamic-slice_fusion.4, f32[1024,2048]{1,0:T(8,128)S(1)} %convert_multiply_fusion), kind=kOutput, calls=%fused_computation.33 | convolution fusion | flops 15044444160 | bytes 30425088 | tf_op jit(solution)/shard_map/crd,cdh->rch/dot_general | solution.py:37
  137.6 112.2 %reduce-scatter.6.cloned.1.call-done = bf16[256,2,2,1792]{3,0,1,2:T(8,128)(2,1)} async-done(((bf16[1024,2,2,1792]{3,0,1,2:T(8,128)(2,1)}), bf16[256,2,2,1792]{3,0,1,2:T(8,128)(2,1)}) %reduce-scatter.6.cloned.1.call-update) | async-done | bytes 3670032 | tf_op jit(solution)/shard_map/reduce_scatter | solution.py:61
  254.9 50.9 %all-gather.6.cloned.1.call-done = bf16[256,2,3584]{2,0,1:T(8,128)(2,1)} async-done(((bf16[256,2,1792]{2,0,1:T(8,128)(2,1)}), bf16[256,2,3584]{2,0,1:T(8,128)(2,1)}) %all-gather.6.cloned.1.call-update) | async-done | bytes 3670032 | tf_op jit(solution)/shard_map/all_gather | solution.py:67
  305.9 26.6 %convolution_bitcast_fusion = f32[256,2,4096]{2,0,1:T(8,128)} fusion(bf16[256,2,3584]{2,0,1:T(8,128)(2,1)} %all-gather.6.cloned.1.call-done, bf16[2,3584,4096]{2,1,0:T(8,128)(2,1)} %param.13), kind=kOutput, calls=%fused_computation.34 | convolution fusion | flops 15032385536 | bytes 70778880 | tf_op jit(solution)/shard_map/rch,chd->rcd/dot_general | solution.py:65
  332.6 144.7 %reduce-scatter.8.cloned.1.call-done = f32[64,2,4096]{2,0,1:T(8,128)} async-done(((f32[256,2,4096]{2,0,1:T(8,128)}), f32[64,2,4096]{2,0,1:T(8,128)}) %reduce-scatter.8.cloned.1.call-update) | async-done | bytes 2097168 | tf_op jit(solution)/shard_map/reduce_scatter | solution.py:71
  482.9 22.2 %all-reduce.12.cloned.1.call-done = f32[64,512]{1,0:T(8,128)} async-done(((f32[64,512]{1,0:T(8,128)}), f32[64,512]{1,0:T(8,128)}) %all-reduce.12.cloned.1.call-update) | async-done | bytes 131088 | tf_op jit(solution)/shard_map/psum | solution.py:31
  515.1 170.2 %all-reduce.14.cloned.1.call-done = f32[4096,512]{1,0:T(8,128)} async-done(((f32[4096,512]{1,0:T(8,128)}), f32[4096,512]{1,0:T(8,128)}) %all-reduce.14.cloned.1.call-update) | async-done | bytes 8388624 | tf_op jit(solution)/shard_map/psum | solution.py:25
  685.3 18.6 convolution_multiply_fusion.6
  704.1 39.9 %all-reduce.16.cloned.1.call-done = f32[512,512]{0,1:T(8,128)} async-done(((f32[512,512]{0,1:T(8,128)}), f32[512,512]{0,1:T(8,128)}) %all-reduce.16.cloned.1.call-update) | async-done | bytes 1048592 | tf_op jit(solution)/shard_map/psum | solution.py:26
  748.0 11.7 cholesky.374
  772.2 11.7 cholesky.393
  784.0 10.2 custom-call.32
  795.8 11.7 cholesky.414
  819.4 11.7 cholesky.431
  836.3 11.7 while.6
  848.0 39.3 %custom-call.34 = f32[4,128,128]{1,2,0:T(8,128)S(1)} custom-call(f32[4,128,128]{2,1,0:T(8,128)S(1)} %get-tuple-element.24), custom_call_target="InvertDiagBlocksLowerTriangular" | custom-call | tf_op jit(solution)/shard_map/triangular_solve/custom-call.3 | solution.py:15
  909.0 12.4 fusion.46
  932.4 21.6 %all-reduce.18.cloned.1.call-done = f32[64,512]{1,0:T(8,128)} async-done(((f32[64,512]{1,0:T(8,128)}), f32[64,512]{1,0:T(8,128)}) %all-reduce.18.cloned.1.call-update) | async-done | bytes 131088 | tf_op jit(solution)/shard_map/psum | solution.py:31
  954.0 10.0 convolution_multiply_fusion.2
  964.1 170.2 %all-reduce.20.cloned.1.call-done = f32[4096,512]{1,0:T(8,128)} async-done(((f32[4096,512]{1,0:T(8,128)}), f32[4096,512]{1,0:T(8,128)}) %all-reduce.20.cloned.1.call-update) | async-done | bytes 8388624 | tf_op jit(solution)/shard_map/psum | solution.py:25
  1134.3 18.6 convolution_multiply_fusion.5
  1153.3 39.6 %all-reduce.22.cloned.1.call-done = f32[512,512]{0,1:T(8,128)} async-done(((f32[512,512]{0,1:T(8,128)}), f32[512,512]{0,1:T(8,128)}) %all-reduce.22.cloned.1.call-update) | async-done | bytes 1048592 | tf_op jit(solution)/shard_map/psum | solution.py:26
  1197.1 11.7 cholesky.446
  1221.3 11.7 cholesky.465
  1234.4 10.0 custom-call.36
  1245.9 11.7 cholesky.486
  1269.6 11.7 cholesky.503
  1286.1 11.7 while.7
  1297.8 39.3 %custom-call.38 = f32[4,128,128]{1,2,0:T(8,128)S(1)} custom-call(f32[4,128,128]{2,1,0:T(8,128)S(1)} %get-tuple-element.25), custom_call_target="InvertDiagBlocksLowerTriangular" | custom-call | tf_op jit(solution)/shard_map/triangular_solve/custom-call.3 | solution.py:15
  1358.6 12.5 fusion.43
  1382.0 21.6 %all-reduce.24.cloned.1.call-done = f32[64,512]{1,0:T(8,128)} async-done(((f32[64,512]{1,0:T(8,128)}), f32[64,512]{1,0:T(8,128)}) %all-reduce.24.cloned.1.call-update) | async-done | bytes 131088 | tf_op jit(solution)/shard_map/psum | solution.py:31
  1403.6 10.2 convolution_multiply_fusion.1
  1413.9 170.2 %all-reduce.26.cloned.1.call-done = f32[4096,512]{1,0:T(8,128)} async-done(((f32[4096,512]{1,0:T(8,128)}), f32[4096,512]{1,0:T(8,128)}) %all-reduce.26.cloned.1.call-update) | async-done | bytes 8388624 | tf_op jit(solution)/shard_map/psum | solution.py:25
  1584.1 18.6 convolution_multiply_fusion.4
  1602.9 39.9 %all-reduce.28.cloned.1.call-done = f32[512,512]{0,1:T(8,128)} async-done(((f32[512,512]{0,1:T(8,128)}), f32[512,512]{0,1:T(8,128)}) %all-reduce.28.cloned.1.call-update) | async-done | bytes 1048592 | tf_op jit(solution)/shard_map/psum | solution.py:26
  1645.8 11.7 cholesky.518
  1668.1 11.7 cholesky.537
  1681.1 10.2 custom-call.40
  1692.0 11.7 cholesky.558
  1714.8 11.7 cholesky.575
  1737.7 39.3 %custom-call.42 = f32[4,128,128]{1,2,0:T(8,128)S(1)} custom-call(f32[4,128,128]{2,1,0:T(8,128)S(1)} %get-tuple-element.26), custom_call_target="InvertDiagBlocksLowerTriangular" | custom-call | tf_op jit(solution)/shard_map/triangular_solve/custom-call.3 | solution.py:15
  1799.1 13.1 fusion.40
  1824.4 21.6 %all-reduce.30.cloned.1.call-done = f32[64,512]{1,0:T(8,128)} async-done(((f32[64,512]{1,0:T(8,128)}), f32[64,512]{1,0:T(8,128)}) %all-reduce.30.cloned.1.call-update) | async-done | bytes 131088 | tf_op jit(solution)/shard_map/psum | solution.py:31
  1846.1 10.2 convolution_multiply_fusion
  1869.4 99.4 %reduce-scatter.10.cloned.1.call-done = f32[32,4096]{1,0:T(8,128)} async-done(((f32[512,4096]{1,0:T(8,128)}), f32[32,4096]{1,0:T(8,128)}) %reduce-scatter.10.cloned.1.call-update) | async-done | bytes 524304
  (192 shorter events, 289.6 us)
Async XLA Ops:
  7.2 31.8 %copy-start = (f32[2,8192]{1,0:T(2,128)S(1)}, f32[2,8192]{1,0:T(2,128)}, u32[]{:S(2)}) copy-start(f32[2,8192]{1,0:T(2,128)} %param.10) | copy-start | bytes 196612
  7.2 78.5 %all-gather.4.cloned.1.call-start = ((), (), s32[]{:S(2)}) async-start(), calls=%async_computation.3 | async-start | bytes 4718592 | tf_op jit(solution)/shard_map/all_gather | solution.py:56
  7.9 241.9 %reduce-scatter.6.cloned.1.call-start = ((), (), s32[]{:S(2)}) async-start(), calls=%async_computation.4 | async-start | bytes 18350080 | tf_op jit(solution)/shard_map/reduce_scatter | solution.py:61
  137.2 168.7 %all-gather.6.cloned.1.call-start = ((), (), s32[]{:S(2)}) async-start(), calls=%async_computation.5 | async-start | bytes 5505024 | tf_op jit(solution)/shard_map/all_gather | solution.py:67
  254.9 222.4 %reduce-scatter.8.cloned.1.call-start = ((), (), s32[]{:S(2)}) async-start(), calls=%async_computation.6 | async-start | bytes 10485760 | tf_op jit(solution)/shard_map/reduce_scatter | solution.py:71
  332.5 172.7 %all-reduce.12.cloned.1.call-start = ((), (), s32[]{:S(2)}) async-start(), calls=%async_computation.7 | async-start | bytes 262144 | tf_op jit(solution)/shard_map/psum | solution.py:31
  477.3 27.9 %copy-start.3 = (f32[64,2,4096]{2,0,1:T(8,128)S(1)}, f32[64,2,4096]{2,0,1:T(8,128)}, u32[]{:S(2)}) copy-start(f32[64,2,4096]{2,0,1:T(8,128)} %reduce-scatter.8.cloned.1.call-done) | copy-start | bytes 6291460
  482.9 202.4 %all-reduce.14.cloned.1.call-start = ((), (), s32[]{:S(2)}) async-start(), calls=%async_computation.8 | async-start | bytes 16777216 | tf_op jit(solution)/shard_map/psum | solution.py:25
  515.0 228.9 %all-reduce.16.cloned.1.call-start = ((), (), s32[]{:S(2)}) async-start(), calls=%async_computation.9 | async-start | bytes 2097152 | tf_op jit(solution)/shard_map/psum | solution.py:26
  703.8 250.2 %all-reduce.18.cloned.1.call-start = ((), (), s32[]{:S(2)}) async-start(), calls=%async_computation.10 | async-start | bytes 262144 | tf_op jit(solution)/shard_map/psum | solution.py:31
  747.0 1.1 copy-start.8
  932.3 201.9 %all-reduce.20.cloned.1.call-start = ((), (), s32[]{:S(2)}) async-start(), calls=%async_computation.11 | async-start | bytes 16777216 | tf_op jit(solution)/shard_map/psum | solution.py:25
  964.1 228.9 %all-reduce.22.cloned.1.call-start = ((), (), s32[]{:S(2)}) async-start(), calls=%async_computation.12 | async-start | bytes 2097152 | tf_op jit(solution)/shard_map/psum | solution.py:26
  1152.9 250.7 %all-reduce.24.cloned.1.call-start = ((), (), s32[]{:S(2)}) async-start(), calls=%async_computation.13 | async-start | bytes 262144 | tf_op jit(solution)/shard_map/psum | solution.py:31
  1196.0 1.1 copy-start.7
  1381.9 202.1 %all-reduce.26.cloned.1.call-start = ((), (), s32[]{:S(2)}) async-start(), calls=%async_computation.14 | async-start | bytes 16777216 | tf_op jit(solution)/shard_map/psum | solution.py:25
  1413.8 228.9 %all-reduce.28.cloned.1.call-start = ((), (), s32[]{:S(2)}) async-start(), calls=%async_computation.15 | async-start | bytes 2097152 | tf_op jit(solution)/shard_map/psum | solution.py:26
  1602.6 243.4 %all-reduce.30.cloned.1.call-start = ((), (), s32[]{:S(2)}) async-start(), calls=%async_computation.16 | async-start | bytes 262144 | tf_op jit(solution)/shard_map/psum | solution.py:31
  1787.6 26.6 %copy-start.2 = (f32[4096,128]{0,1:T(8,128)}, f32[4096,128]{0,1:T(8,128)S(1)}, u32[]{:S(2)}) copy-start(f32[4096,128]{0,1:T(8,128)S(1)} %fusion.97) | copy-start | bytes 6291460
  1799.1 15.2 copy-start.5
  1812.2 3.4 copy-start.4
  1814.2 1.3 copy-start.6
  1824.4 144.5 %reduce-scatter.10.cloned.1.call-start = ((), (), s32[]{:S(2)}) async-start(), calls=%async_computation.17 | async-start | bytes 8912896
  1865.2 103.6 %copy-start.1 = (f32[2,8192]{1,0:T(2,128)S(1)}, f32[2,8192]{1,0:T(2,128)}, u32[]{:S(2)}) copy-start(f32[2,8192]{1,0:T(2,128)} %param.10) | copy-start | bytes 196612
Sparse Core Ops, SparseCore 0:
  10.1 75.5 all-gather.3
  137.3 112.4 reduce-scatter.5
  255.0 50.8 all-gather.5
  332.6 144.6 reduce-scatter.7
  483.0 22.1 all-reduce.11
  515.1 170.0 all-reduce.13
  704.0 39.9 all-reduce.15
  932.5 21.5 all-reduce.17
  964.2 170.0 all-reduce.19
  1153.0 39.9 all-reduce.21
  1382.0 21.5 all-reduce.23
  1413.9 170.0 all-reduce.25
  1602.8 39.9 all-reduce.27
  1824.5 21.5 all-reduce.29
  1865.3 103.4 reduce-scatter.9
where the time goes:
time: 1990 us; the launch traced here: 1980 us
  waiting for transfers between devices  1170 us (59%)
  other arithmetic  385 us (19%)
  matrix products  316 us (16%)
  local copies, waits for them, and re-layouts  49.2 us (2%)
  blocking collectives  29.7 us (1%)
  between operations  22.3 us (1%)
    psum x3, waiting for transfers between devices, orthonormal(): summed = lax.psum(partial_value, ('mp', 'dp'))  511 us
    another operation x44, other arithmetic, orthonormal_from(): lower_factor = jnp.linalg.cholesky(gram_total)  237 us
    reduce_scatter x1, waiting for transfers between devices, on_device(): lax.psum_scatter(partial_out, 'mp', scatter_dimension=0, tiled=True)  145 us
    another operation x8, other arithmetic, orthonormal_from(): lax.linalg.triangular_solve(lower_factor, matrix, left_side=False, lower=...  125 us
    psum x3, waiting for transfers between devices, orthonormal(): gram_total = lax.psum(gram_of(summed), 'tensor')  119 us
    reduce_scatter x1, waiting for transfers between devices, on_device(): lax.psum_scatter(all_terms.astype(jnp.bfloat16), 'dp', scatter_dimension=...  112 us
    another operation x21, matrix products, orthonormal_from(): lax.linalg.triangular_solve(lower_factor, matrix, left_side=False, lower=...  109 us
    unnamed x16, waiting for transfers between devices  100 us
  transfers between devices with their start and end apart: 15, of which 15 were waited for; matrix products, arithmetic and copies ran while one was open for 0% of the time, Pallas kernels for 0%

commit v1 on v0

v1 whole, which is shorter than its diff:
```python
import functools

import jax
import jax.numpy as jnp
from jax import lax
from jax.experimental import pallas as pl
from jax.experimental.pallas import tpu as pltpu
from jax.sharding import PartitionSpec as P

EPSILON = 1e-05
HIGH = lax.Precision.HIGH
HIGHEST = lax.Precision.HIGHEST
F32 = jnp.float32
BF16 = jnp.bfloat16
LEAF = 128


def swap(value, axis, bit):
    pairs = [(i, i ^ bit) for i in range(lax.axis_size(axis))]
    return lax.ppermute(value, axis, pairs)


def bits_of(axis):
    return [(axis, 1 << b) for b in range(lax.axis_size(axis).bit_length() - 1)]


def piece(value, index):
    return lax.dynamic_index_in_dim(value, index, 0, keepdims=False)


def leaf_inverse(block):
    size = block.shape[0]
    groups = [block[8 * g : 8 * g + 8, :] for g in range(size // 8)]
    lane = lax.broadcasted_iota(jnp.int32, (8, size), 1)
    sub = lax.broadcasted_iota(jnp.int32, (8, size), 0)
    pivots = []
    for j in range(size):
        home, row_at = divmod(j, 8)
        row = groups[home][row_at : row_at + 1, :]
        pivot = row[:, j : j + 1]
        inverse = 1.0 / pivot
        here = lane == j
        scaled = jnp.where(here, inverse, jnp.broadcast_to(row * inverse, (8, size)))
        for g in range(home, size // 8):
            old = groups[g]
            column = jnp.broadcast_to(old[:, j : j + 1], (8, size))
            new = jnp.where(here, 0.0, old) - column * scaled
            groups[g] = jnp.where(sub > row_at, new, old) if g == home else new
    out = []
    for g in range(size // 8):
        diagonal = jnp.sum(jnp.where(lane == sub + 8 * g, groups[g], 0.0), axis=1, keepdims=True)
        unit = jnp.where(lane == sub + 8 * g, 1.0, jnp.where(lane < sub + 8 * g, groups[g], 0.0))
        out.append(unit * lax.rsqrt(diagonal))
    return jnp.concatenate(out, axis=0)


def factor_kernel(gram_ref, out_ref, work_ref):
    size = gram_ref.shape[0]
    work_ref[...] = gram_ref[...]
    lane = lax.broadcasted_iota(jnp.int32, (LEAF, size), 1)

    def step(k, _):
        start = pl.multiple_of(k * LEAF, LEAF)
        rows = work_ref[pl.ds(start, LEAF), :]
        inverse = leaf_inverse(work_ref[pl.ds(start, LEAF), pl.ds(start, LEAF)])
        panel = jnp.dot(inverse, rows, precision=HIGHEST, preferred_element_type=F32)
        out_ref[pl.ds(start, LEAF), :] = jnp.where(lane < start, panel, 0.0)
        out_ref[pl.ds(start, LEAF), pl.ds(start, LEAF)] = inverse
        after = jnp.where(lane >= start + LEAF, panel, 0.0)
        work_ref[pl.ds(start, LEAF), :] = panel
        work_ref[pl.ds(start, LEAF), pl.ds(start, LEAF)] = inverse
        wide = work_ref[pl.ds(start, LEAF), :]
        work_ref[:, pl.ds(start, LEAF)] = jnp.zeros((size, LEAF), F32)
        work_ref[...] -= lax.dot_general(
            after, wide, (((0,), (0,)), ((), ())), precision=HIGHEST, preferred_element_type=F32
        )
        return 0

    lax.fori_loop(0, size // LEAF, step, 0)


def factor_inverse(gram):
    size = gram.shape[0]
    return pl.pallas_call(
        factor_kernel,
        out_shape=jax.ShapeDtypeStruct((size, size), F32),
        in_specs=[pl.BlockSpec(memory_space=pltpu.VMEM)],
        out_specs=pl.BlockSpec(memory_space=pltpu.VMEM),
        scratch_shapes=[pltpu.VMEM((size, size), F32)],
        cost_estimate=pl.CostEstimate(
            flops=100_000_000_000, bytes_accessed=8 * size * size, transcendentals=0
        ),
        name="factor_inverse",
    )(gram)


def down_kernel(hidden_ref, weight_ref, out_ref):
    out_ref[0] = jnp.dot(
        hidden_ref[...], weight_ref[0], preferred_element_type=F32
    ).astype(out_ref.dtype)


def down_project(hidden, down_weight, copy, pieces):
    rows, units = hidden.shape
    width = down_weight.shape[2] // pieces
    tile = min(width, 512)
    steps = width // tile
    return pl.pallas_call(
        down_kernel,
        grid=(pieces, steps),
        in_specs=[
            pl.BlockSpec((rows, units), lambda p, s: (0, 0)),
            pl.BlockSpec((1, units, tile), lambda p, s: (copy, 0, p * steps + s)),
        ],
        out_specs=pl.BlockSpec((1, rows, tile), lambda p, s: (p, 0, s)),
        out_shape=jax.ShapeDtypeStruct((pieces, rows, width), BF16),
        cost_estimate=pl.CostEstimate(
            flops=2 * rows * units * width * pieces,
            bytes_accessed=2 * units * width * pieces,
            transcendentals=0,
        ),
        name="down_project",
    )(hidden, down_weight)


def scatter_step(value, axis, bit):
    side = (lax.axis_index(axis) // bit) % 2
    halves = value.reshape((2, value.shape[0] // 2) + value.shape[1:])
    received = swap(piece(halves, 1 - side), axis, bit)
    return (piece(halves, side).astype(F32) + received.astype(F32)).astype(value.dtype)


def gather_step(value, axis, bit):
    side = (lax.axis_index(axis) // bit) % 2
    received = swap(value, axis, bit)
    first = jnp.where(side == 0, value, received)
    second = jnp.where(side == 0, received, value)
    return jnp.concatenate((first, second), axis=0)


def all_reduce(parts, orders):
    values = list(parts)
    for stage in range(len(orders[0])):
        values = [scatter_step(v, *o[stage]) for v, o in zip(values, orders, strict=True)]
    for stage in reversed(range(len(orders[0]))):
        values = [gather_step(v, *o[stage]) for v, o in zip(values, orders, strict=True)]
    return values


def split_dot(left, right):
    high = right.astype(BF16)
    low = (right - high.astype(F32)).astype(BF16)
    both = jnp.dot(left, jnp.concatenate((high, low), axis=1), preferred_element_type=F32)
    width = right.shape[1]
    return both[:, :width] + both[:, width:]


def on_device(tokens, norm_gain, gate_weight, up_weight, down_weight, sketch):
    dp, mp, tensor = lax.axis_size("dp"), lax.axis_size("mp"), lax.axis_size("tensor")
    me = lax.axis_index("dp")
    tokens_all = tokens.shape[0] * mp * tensor
    feature_count = tokens.shape[1]
    width = feature_count * dp
    group = tokens_all // dp

    local_gain = lax.dynamic_slice_in_dim(norm_gain, me * feature_count, feature_count, 1)
    local_values = tokens.astype(F32)
    local_total = lax.psum(jnp.sum(local_values * local_values, axis=1), "dp")
    local_root = lax.rsqrt(local_total / width + EPSILON)
    root_all = lax.all_gather(local_root, ("mp", "tensor"), axis=0, tiled=True)
    token_groups = lax.all_gather(tokens, ("mp", "tensor"), axis=0, tiled=True)
    token_groups = token_groups.reshape(dp, group, feature_count)
    root_groups = root_all.reshape(dp, group)

    def normed_rows(copy, offsets):
        rows = jnp.concatenate([piece(token_groups, me ^ j) for j in offsets], axis=0)
        roots = jnp.concatenate([piece(root_groups, me ^ j) for j in offsets], axis=0)
        return (rows.astype(F32) * roots[:, None] * local_gain[copy][None, :]).astype(BF16)

    def project(copy, offsets):
        rows = normed_rows(copy, offsets)
        gate = jnp.dot(rows, gate_weight[copy], preferred_element_type=F32).astype(BF16)
        up = jnp.dot(rows, up_weight[copy], preferred_element_type=F32).astype(BF16)
        return gate, up

    def hidden_of(copy):
        order = list(range(dp))
        held = None
        bit = 1
        while bit < dp:
            away = [j for j in order if j & bit]
            order = [j for j in order if not j & bit]
            if held is None:
                sent = project(copy, away)
                received = tuple(swap(v, "dp", bit) for v in sent)
                held = project(copy, order)
            else:
                split = held[0].shape[0] // 2
                received = tuple(swap(v[split:], "dp", bit) for v in held)
                held = tuple(v[:split] for v in held)
            held = tuple(a.astype(F32) + b.astype(F32) for a, b in zip(held, received, strict=True))
            bit *= 2
            if bit < dp:
                held = tuple(v.astype(BF16) for v in held)
        gate, up = held
        return (jax.nn.silu(gate) * up).astype(BF16)

    def gather_units(hidden):
        if tensor != 2:
            return lax.all_gather(hidden, "tensor", axis=1, tiled=True)
        other = swap(hidden, "tensor", 1)
        first = lax.axis_index("tensor") == 0
        return jnp.concatenate(
            (jnp.where(first, hidden, other), jnp.where(first, other, hidden)), axis=1
        )

    def acts_of(copy):
        hidden = gather_units(hidden_of(copy))
        partial = down_project(hidden, down_weight, copy, mp)
        summed = lax.psum_scatter(partial, "mp", scatter_dimension=0, tiled=False)
        blocks = summed.reshape(group, dp, -1).transpose(1, 0, 2)
        own = piece(blocks, me)
        arrived = [own] + [
            lax.ppermute(piece(blocks, me ^ j), "dp", [(i, i ^ j) for i in range(dp)])
            for j in range(1, dp)
        ]
        stacked = jnp.stack(arrived)
        bit = 1
        while bit < dp:
            turned = jnp.stack([stacked[j ^ bit] for j in range(dp)])
            stacked = jnp.where((me // bit) % 2 == 1, turned, stacked)
            bit *= 2
        return stacked.reshape(tokens_all, -1)

    inst = acts_of(1)
    base = acts_of(0)
    share = inst.shape[1]
    spot = lax.axis_index(("mp", "dp"))
    sketch_rows = lax.dynamic_slice_in_dim(sketch, spot * share, share, 0)
    rank = sketch.shape[1]

    def outer(value):
        return lax.dot_general(
            value, value, (((1,), (1,)), ((), ())), preferred_element_type=F32
        ).astype(BF16)

    first_inner = jnp.dot(inst, sketch_rows, preferred_element_type=F32).astype(BF16)
    base_outer = outer(base)
    core = bits_of("dp")[:1]
    far = bits_of("dp")[1:]
    ways = [
        core + far + bits_of("tensor") + bits_of("mp"),
        core + bits_of("tensor") + bits_of("mp") + far,
        core + bits_of("mp") + far + bits_of("tensor"),
    ]
    half = tokens_all // 2
    inner, outer_a, outer_b = all_reduce(
        (first_inner, base_outer[:, :half], base_outer[:, half:]), ways
    )
    base_outer = jnp.concatenate((outer_a, outer_b), axis=1)
    inst_outer = lax.psum(outer(inst), ("mp", "dp", "tensor"))

    scale = 1.0 / (tokens_all * tokens_all * width)

    def round_of(outer_matrix, inner_sums):
        moved = split_dot(outer_matrix, inner_sums)
        gram = lax.dot_general(
            inner_sums, moved, (((0,), (0,)), ((), ())), precision=HIGH
        ) * scale
        return moved, factor_inverse(gram)

    def turn(matrix, inverse):
        return lax.dot_general(matrix, inverse, (((1,), (1,)), ((), ())), precision=HIGH) / tokens_all

    moved, inverse = round_of(base_outer, inner.astype(F32))
    second_inner = turn(moved, inverse)
    moved, inverse = round_of(inst_outer, second_inner)
    third_inner = turn(moved, inverse)
    moved, inverse = round_of(base_outer, third_inner)
    basis_inner = turn(third_inner, inverse).astype(BF16)
    last_inner = (turn(moved, inverse) / tokens_all).astype(BF16)

    def outputs(inner_sums, acts):
        return lax.dot_general(
            inner_sums, acts, (((0,), (0,)), ((), ())), preferred_element_type=F32
        ).astype(BF16)

    both = jnp.stack((outputs(basis_inner, base), outputs(last_inner, inst)))
    shares = mp * dp
    both = both.reshape(2, shares, rank // shares, share).transpose(1, 0, 2, 3)
    both = lax.all_to_all(both, ("mp", "dp"), 0, 0, tiled=True)
    both = both.transpose(1, 0, 3, 2).reshape(2, shares * share, rank // shares).astype(F32)
    return both[0], both[1]


def solution(mesh):
    return jax.shard_map(
        on_device,
        mesh=mesh,
        in_specs=(
            P(("mp", "tensor"), "dp"),
            P(),
            P(None, "dp", ("mp", "tensor")),
            P(None, "dp", ("mp", "tensor")),
            P(None, "mp", "tensor"),
            P("tensor", None),
        ),
        out_specs=(P("tensor", ("mp", "dp")), P("tensor", ("mp", "dp"))),
        check_vma=False,
    )
```

time: 1990 us -> 683 us (0.34)
  waiting for transfers between devices: 1170 us -> 189 us
  other arithmetic: 385 us -> 14.5 us
  Pallas kernels: 0 us -> 257 us
  matrix products: 316 us -> 90.8 us
  starting transfers between devices: 1.72 us -> 37.2 us
  local copies, waits for them, and re-layouts: 49.2 us -> 22.7 us
    psum x10 -> x1, waiting for transfers between devices: 717 us -> 0.01 us  [on_device(): inst_outer = lax.psum(outer(inst), ('mp', 'dp', 'tensor'))]
    another operation x53 -> x0, other arithmetic: 371 us -> none  [the longest x44 237 us: orthonormal_from(): lower_factor = jnp.linalg.cholesky(gram_total)]
    pallas_call x0 -> x5, Pallas kernels: none -> 257 us  [the longest x3 224 us: factor_inverse(): pl.pallas_call(factor_kernel, out_shape=jax.ShapeDtypeStruct((size, size)...]
    reduce_scatter x2, waiting for transfers between devices: 257 us -> 44.8 us  [acts_of(): summed = lax.psum_scatter(partial, 'mp', scatter_dimension=0, tiled=False)]
    another operation x39 -> x0, matrix products: 122 us -> none  [the longest x21 109 us: orthonormal_from(): lax.linalg.triangular_solve(lower_factor, matrix, left_side=False, lower=...]
    dot_general x14 -> x23, matrix products: 194 us -> 90.8 us  [the longest x4 30.8 us: project(): jnp.dot(rows, gate_weight[copy], preferred_element_type=F32).astype(BF16)]
    unnamed x16 -> x4, waiting for transfers between devices: 100 us -> 0.73 us
    ppermute x0 -> x46, waiting for transfers between devices: none -> 98.8 us  [the longest x40 92.6 us: swap(): return lax.ppermute(value, axis, pairs)]
  transfers between devices with their start and end apart: 15 -> 50, of which waited for: 15 -> 29; matrix products, arithmetic and copies ran while one was open for 0% -> 12% of each run, Pallas kernels for 0% -> 16%
where the time goes in v1:
time: 683 us; the launch traced here: 673 us
  Pallas kernels  257 us (38%)
  waiting for transfers between devices  189 us (28%)
  matrix products  90.8 us (13%)
  blocking collectives  47.5 us (7%)
  starting transfers between devices  37.2 us (5%)
  local copies, waits for them, and re-layouts  22.7 us (3%)
  between operations  15.1 us (2%)
  other arithmetic  14.5 us (2%)
    pallas_call x3, Pallas kernels, factor_inverse(): pl.pallas_call(factor_kernel, out_shape=jax.ShapeDtypeStruct((size, size)...  224 us
    ppermute x40, waiting for transfers between devices, swap(): return lax.ppermute(value, axis, pairs)  92.6 us
    reduce_scatter x2, waiting for transfers between devices, acts_of(): summed = lax.psum_scatter(partial, 'mp', scatter_dimension=0, tiled=False)  44.8 us
    all_gather x1, waiting for transfers between devices, on_device(): token_groups = lax.all_gather(tokens, ('mp', 'tensor'), axis=0, tiled=True)  44.6 us
    ppermute x40, starting transfers between devices, swap(): return lax.ppermute(value, axis, pairs)  32.9 us
    pallas_call x2, Pallas kernels, down_project(): pl.pallas_call(down_kernel, grid=(pieces, steps), in_specs=[pl.BlockSpec(...  32.3 us
    dot_general x4, matrix products, project(): jnp.dot(rows, gate_weight[copy], preferred_element_type=F32).astype(BF16)  30.8 us
    all_gather x1, blocking collectives, on_device(): root_all = lax.all_gather(local_root, ('mp', 'tensor'), axis=0, tiled=True)  21.4 us
  transfers between devices with their start and end apart: 50, of which 29 were waited for; matrix products, arithmetic and copies ran while one was open for 12% of the time, Pallas kernels for 16%

profile of v1, /device:TPU:0, one launch (start us, length us, event | category | flops | bytes accessed | tf_op | source)
XLA Modules:
  0.0 673.2 jit_solution(13330883801414590877)
XLA Ops:
  9.2 8.4 %psum.14 = f32[128]{0:T(128)S(1)} all-reduce(f32[128]{0:T(128)S(1)} %multiply_reduce_fusion), channel_id=1, replica_groups=mesh['mp'=4,'dp'=4,'tensor'=2] {'dp'}, use_global_device_ids=true, to_apply=%region_1.0 | all-reduce | flops 128 | bytes 1024 | tf_op jit(solution)/shard_map/psum | solution.py:168
  17.6 21.4 %all-gather = f32[8,1,128]{2,1,0:T(1,128)S(1)} all-gather(f32[1,1,128]{2,1,0:T(1,128)S(1)} %rsqrt_bitcast_fusion), channel_id=1, replica_groups=mesh['mp'=4,'dp'=4,'tensor'=2] {'mp','tensor'}, dimensions={0}, use_global_device_ids=true | all-gather | bytes 4608 | tf_op jit(solution)/shard_map/all_gather | solution.py:170
  41.1 44.6 %all-gather.3.cloned.1.call-done = bf16[1024,2048]{1,0:T(8,128)(2,1)} async-done(((bf16[128,2048]{1,0:T(8,128)(2,1)}), bf16[1024,2048]{1,0:T(8,128)(2,1)}) %all-gather.3.cloned.1.call-update) | async-done | bytes 4194320 | tf_op jit(solution)/shard_map/all_gather | solution.py:171
  85.7 2.6 dynamic-slice_bitcast_fusion.3
  88.3 7.3 %fusion.45 = bf16[512,1792]{1,0:T(8,128)(2,1)S(1)} fusion(bf16[2,2048,1792]{2,1,0:T(8,128)(2,1)} %param.9, f32[2048]{0:T(1024)S(1)} %bitcast.287, f32[512]{0:T(512)S(1)} %pad_maximum_fusion.19, bf16[256,2048]{1,0:T(8,128)(2,1)S(1)} %get-tuple-element.3, bf16[256,2048]{1,0:T(8,128)(2,1)S(1)} %get-tuple-element.4), kind=kOutput, calls=%fused_computation.41 | convolution fusion | flops 3766353920 | bytes 11282432 | tf_op jit(solution)/shard_map/dot_general | solution.py:183
  95.7 7.3 %fusion.39 = bf16[512,1792]{1,0:T(8,128)(2,1)S(1)} fusion(bf16[2,2048,1792]{2,1,0:T(8,128)(2,1)} %param.8, f32[2048]{0:T(1024)S(1)} %bitcast.288, f32[512]{0:T(512)S(1)} %pad_maximum_fusion.19, bf16[256,2048]{1,0:T(8,128)(2,1)S(1)} %get-tuple-element.3, bf16[256,2048]{1,0:T(8,128)(2,1)S(1)} %get-tuple-element.4), kind=kOutput, calls=%fused_computation.39 | convolution fusion | flops 3766353920 | bytes 11282432 | tf_op jit(solution)/shard_map/dot_general | solution.py:182
  103.4 4.0 fusion.33
  107.6 8.3 %fusion.27 = bf16[512,1792]{1,0:T(8,128)(2,1)} fusion(bf16[2,2048,1792]{2,1,0:T(8,128)(2,1)} %param.8, f32[512]{0:T(512)S(1)} %pad_maximum_fusion.19, f32[2048]{0:T(1024)S(1)} %bitcast.284, bf16[256,2048]{1,0:T(8,128)(2,1)S(1)} %get-tuple-element.3, bf16[256,2048]{1,0:T(8,128)(2,1)S(1)} %get-tuple-element.4), kind=kOutput, calls=%fused_computation.35 | convolution fusion | flops 3766353920 | bytes 11282432 | tf_op jit(solution)/shard_map/dot_general | solution.py:182
  116.3 4.5 add_convert_fusion
  122.4 7.6 %add_convert_fusion.1 = bf16[512,1792]{1,0:T(8,128)(2,1)S(1)} fusion(bf16[512,1792]{1,0:T(8,128)(2,1)} %collective-permute-done.8, bf16[2,2048,1792]{2,1,0:T(8,128)(2,1)} %param.8, f32[2048]{0:T(1024)S(1)} %bitcast.290, f32[512]{0:T(512)S(1)} %pad_maximum_fusion.18, bf16[256,2048]{1,0:T(8,128)(2,1)S(1)} %get-tuple-element.5, ...), kind=kOutput, calls=%fused_computation.31 | convolution fusion | flops 3770023936 | bytes 13117440 | tf_op jit(solution)/shard_map/dot_general | solution.py:182
  130.8 5.5 add_convert_fusion.2
  137.9 6.3 collective-permute-done.11
  144.2 19.7 %collective-permute-done.9 = bf16[256,1792]{1,0:T(8,128)(2,1)S(1)} collective-permute-done((bf16[256,1792]{1,0:T(8,128)(2,1)S(1)}, bf16[256,1792]{1,0:T(8,128)(2,1)S(1)}, u32[]{:S(2)}, u32[]{:S(2)}) %collective-permute-start.9) | collective-permute-done | bytes 917536 | tf_op jit(solution)/shard_map/ppermute | solution.py:20
  165.2 7.6 %add_convert_fusion.3 = bf16[512,1792]{1,0:T(8,128)(2,1)S(1)} fusion(bf16[512,1792]{1,0:T(8,128)(2,1)} %collective-permute-done, bf16[2,2048,1792]{2,1,0:T(8,128)(2,1)} %param.8, f32[2048]{0:T(1024)S(1)} %bitcast.286, f32[512]{0:T(512)S(1)} %pad_maximum_fusion.18, bf16[256,2048]{1,0:T(8,128)(2,1)S(1)} %get-tuple-element.5, ...), kind=kOutput, calls=%fused_computation.33 | convolution fusion | flops 3770023936 | bytes 13117440 | tf_op jit(solution)/shard_map/dot_general | solution.py:182
  175.4 10.0 %collective-permute-done.12 = bf16[256,1792]{1,0:T(8,128)(2,1)S(1)} collective-permute-done((bf16[256,1792]{1,0:T(8,128)(2,1)S(1)}, bf16[256,1792]{1,0:T(8,128)(2,1)S(1)}, u32[]{:S(2)}, u32[]{:S(2)}) %collective-permute-start.12) | collective-permute-done | bytes 917536 | tf_op jit(solution)/shard_map/ppermute | solution.py:20
  186.9 16.1 %down_project.3 = bf16[4,256,1024]{2,1,0:T(8,128)(2,1)} custom-call(bf16[256,3584]{1,0:T(8,128)(2,1)} %pad_maximum_fusion.3.hidden_ref, bf16[2,3584,4096]{2,1,0:T(8,128)(2,1)} %weight_ref.3), custom_call_target="tpu_custom_call" | custom-call | flops 7516192768 | bytes 29360128 | tf_op jit(solution)/shard_map/down_project/pallas_call | solution.py:108
  203.1 2.5 multiply_convert_fusion.8
  206.2 20.3 %collective-permute-done.4 = bf16[256,1792]{1,0:T(8,128)(2,1)S(1)} collective-permute-done((bf16[256,1792]{1,0:T(8,128)(2,1)S(1)}, bf16[256,1792]{1,0:T(8,128)(2,1)S(1)}, u32[]{:S(2)}, u32[]{:S(2)}) %collective-permute-start.4) | collective-permute-done | bytes 917536 | tf_op jit(solution)/shard_map/ppermute | solution.py:20
  228.1 16.2 %down_project.2 = bf16[4,256,1024]{2,1,0:T(8,128)(2,1)} custom-call(bf16[256,3584]{1,0:T(8,128)(2,1)} %pad_maximum_fusion.2.hidden_ref, bf16[2,3584,4096]{2,1,0:T(8,128)(2,1)} %weight_ref.3), custom_call_target="tpu_custom_call" | custom-call | flops 7516192768 | bytes 29360128 | tf_op jit(solution)/shard_map/down_project/pallas_call | solution.py:108
  247.0 43.7 %reduce-scatter.3.cloned.1.call-done = bf16[1,256,1024]{2,1,0:T(8,128)(2,1)} async-done(((bf16[4,256,1024]{2,1,0:T(8,128)(2,1)}), bf16[1,256,1024]{2,1,0:T(8,128)(2,1)}) %reduce-scatter.3.cloned.1.call-update) | async-done | bytes 524304 | tf_op jit(solution)/shard_map/reduce_scatter | solution.py:220
  292.2 2.2 constant_dynamic-slice_fusion.3
  299.8 2.7 collective-permute-done.6
  305.5 2.0 collective-permute-done.14
  311.7 2.1 convolution_convert_fusion.1
  321.2 4.3 collective-permute-done.37
  327.2 2.8 collective-permute-done.27
  330.0 1.9 collective-permute-start.28
  334.3 7.2 %collective-permute-done.28 = bf16[128,512]{1,0:T(8,128)(2,1)S(1)} collective-permute-done((bf16[128,512]{1,0:T(8,128)(2,1)S(1)}, bf16[128,512]{1,0:T(8,128)(2,1)S(1)}, u32[]{:S(2)}, u32[]{:S(2)}) %collective-permute-start.28) | collective-permute-done | bytes 131104 | tf_op jit(solution)/shard_map/ppermute | solution.py:20
  361.7 4.3 collective-permute-done.22
  369.9 2.6 collective-permute-done.23
  372.9 3.2 collective-permute-done.34
  376.3 2.7 collective-permute-done.24
  381.4 2.6 fusion.56
  384.0 2.0 copy-done.8
  386.0 2.3 convolution_multiply_fusion.gram_ref
  388.3 74.6 %factor_inverse.3 = f32[512,512]{1,0:T(8,128)} custom-call(f32[512,512]{1,0:T(8,128)} %convolution_multiply_fusion.gram_ref), custom_call_target="tpu_custom_call" | custom-call | flops 99999997952 | bytes 2097152 | tf_op jit(solution)/shard_map/factor_inverse/pallas_call | solution.py:84
  462.9 5.4 multiply_convert_fusion.6
  468.3 4.2 fusion.62
  472.5 2.0 copy-done.4
  474.5 2.8 fusion.81.gram_ref
  477.4 75.0 %factor_inverse.4 = f32[512,512]{1,0:T(8,128)} custom-call(f32[512,512]{1,0:T(8,128)} %fusion.81.gram_ref), custom_call_target="tpu_custom_call" | custom-call | flops 99999997952 | bytes 2097152 | tf_op jit(solution)/shard_map/factor_inverse/pallas_call | solution.py:84
  552.4 4.5 multiply_convert_fusion.9
  556.9 2.4 fusion.66
  559.3 2.0 copy-done.5
  561.3 2.8 fusion.78.gram_ref
  564.1 74.7 %factor_inverse.5 = f32[512,512]{1,0:T(8,128)} custom-call(f32[512,512]{1,0:T(8,128)} %fusion.78.gram_ref), custom_call_target="tpu_custom_call" | custom-call | flops 99999997952 | bytes 2097152 | tf_op jit(solution)/shard_map/factor_inverse/pallas_call | solution.py:84
  638.9 4.4 multiply_convert_fusion.4
  646.8 17.8 %all_to_all.5 = bf16[16,2,32,256]{3,2,1,0:T(8,128)(2,1)S(1)} all-to-all(bf16[16,2,32,256]{3,2,1,0:T(8,128)(2,1)S(1)} %maximum_bitcast_fusion), channel_id=1, replica_groups=mesh['mp'=4,'dp'=4,'tensor'=2] {'mp','dp'}, dimensions={0} | all-to-all | bytes 1048576 | tf_op jit(solution)/shard_map/all_to_all | solution.py:291
  (231 shorter events, 76.9 us)
Async XLA Ops:
  7.2 78.5 %all-gather.3.cloned.1.call-start = ((), (), s32[]{:S(2)}) async-start(), calls=%async_computation.3 | async-start | bytes 4718592 | tf_op jit(solution)/shard_map/all_gather | solution.py:171
  7.9 237.7 %reduce-scatter.5.cloned.1.call-start = ((), (), s32[]{:S(2)}) async-start(), calls=%async_computation.6 | async-start | bytes 2621440 | tf_op jit(solution)/shard_map/reduce_scatter | solution.py:220
  95.6 20.7 %collective-permute-start.10 = (bf16[512,1792]{1,0:T(8,128)(2,1)S(1)}, bf16[512,1792]{1,0:T(8,128)(2,1)S(1)}, u32[]{:S(2)}, u32[]{:S(2)}) collective-permute-start(bf16[512,1792]{1,0:T(8,128)(2,1)S(1)} %fusion.45), channel_id=1, source_target_pairs={{0,2},{2,0},{4,6},{6,4},{1,3},{3,1},{5,7},{7,5},{8,10},{10,8},{12,... | collective-permute-start | bytes 5505032 | tf_op jit(solution)/shard_map/ppermute | solution.py:20
  102.9 19.5 %collective-permute-start.8 = (bf16[512,1792]{1,0:T(8,128)(2,1)S(1)}, bf16[512,1792]{1,0:T(8,128)(2,1)}, u32[]{:S(2)}, u32[]{:S(2)}) collective-permute-start(bf16[512,1792]{1,0:T(8,128)(2,1)S(1)} %fusion.39), channel_id=1, source_target_pairs={{0,2},{2,0},{4,6},{6,4},{1,3},{3,1},{5,7},{7,5},{8,10},{10,8},{12,... | collective-permute-start | bytes 5505032 | tf_op jit(solution)/shard_map/ppermute | solution.py:20
  107.4 23.4 %collective-permute-start.2 = (bf16[512,1792]{1,0:T(8,128)(2,1)S(1)}, bf16[512,1792]{1,0:T(8,128)(2,1)}, u32[]{:S(2)}, u32[]{:S(2)}) collective-permute-start(bf16[512,1792]{1,0:T(8,128)(2,1)S(1)} %fusion.33), channel_id=1, source_target_pairs={{0,2},{2,0},{4,6},{6,4},{1,3},{3,1},{5,7},{7,5},{8,10},{10,8},{12,... | collective-permute-start | bytes 5505032 | tf_op jit(solution)/shard_map/ppermute | solution.py:20
  116.0 49.3 %collective-permute-start = (bf16[512,1792]{1,0:T(8,128)(2,1)}, bf16[512,1792]{1,0:T(8,128)(2,1)}, u32[]{:S(2)}, u32[]{:S(2)}) collective-permute-start(bf16[512,1792]{1,0:T(8,128)(2,1)} %fusion.27), channel_id=1, source_target_pairs={{0,2},{2,0},{4,6},{6,4},{1,3},{3,1},{5,7},{7,5},{8,10},{10,8},{12,... | collective-permute-start | bytes 5505032 | tf_op jit(solution)/shard_map/ppermute | solution.py:20
  120.9 23.3 %collective-permute-start.11 = (bf16[256,1792]{1,0:T(8,128)(2,1)S(1)}, bf16[256,1792]{1,0:T(8,128)(2,1)S(1)}, u32[]{:S(2)}, u32[]{:S(2)}) collective-permute-start(bf16[256,1792]{1,0:T(8,128)(2,1)S(1)} %slice.137), channel_id=1, source_target_pairs={{0,4},{2,6},{4,0},{6,2},{1,5},{3,7},{5,1},{7,3},{8,12},{10,14},{12... | collective-permute-start | bytes 2752520 | tf_op jit(solution)/shard_map/ppermute | solution.py:20
  130.1 33.7 %collective-permute-start.9 = (bf16[256,1792]{1,0:T(8,128)(2,1)S(1)}, bf16[256,1792]{1,0:T(8,128)(2,1)S(1)}, u32[]{:S(2)}, u32[]{:S(2)}) collective-permute-start(bf16[256,1792]{1,0:T(8,128)(2,1)S(1)} %slice.135), channel_id=1, source_target_pairs={{0,4},{2,6},{4,0},{6,2},{1,5},{3,7},{5,1},{7,3},{8,12},{10,14},{12... | collective-permute-start | bytes 2752520 | tf_op jit(solution)/shard_map/ppermute | solution.py:20
  136.4 66.8 %collective-permute-start.3 = (bf16[256,1792]{1,0:T(8,128)(2,1)S(1)}, bf16[256,1792]{1,0:T(8,128)(2,1)}, u32[]{:S(2)}, u32[]{:S(2)}) collective-permute-start(bf16[256,1792]{1,0:T(8,128)(2,1)S(1)} %slice.131), channel_id=1, source_target_pairs={{0,4},{2,6},{4,0},{6,2},{1,5},{3,7},{5,1},{7,3},{8,12},{10,14},{12... | collective-permute-start | bytes 2752520 | tf_op jit(solution)/shard_map/ppermute | solution.py:20
  164.6 20.8 %collective-permute-start.12 = (bf16[256,1792]{1,0:T(8,128)(2,1)S(1)}, bf16[256,1792]{1,0:T(8,128)(2,1)S(1)}, u32[]{:S(2)}, u32[]{:S(2)}) collective-permute-start(bf16[256,1792]{1,0:T(8,128)(2,1)S(1)} %multiply_convert_fusion.7), channel_id=1, source_target_pairs={{0,1},{1,0},{2,3},{3,2},{4,5},{5,4},{6,7},{7,6},{8,9},{9,8},{10,11... | collective-permute-start | bytes 2752520 | tf_op jit(solution)/shard_map/ppermute | solution.py:20
  173.9 29.2 %collective-permute-start.1 = (bf16[256,1792]{1,0:T(8,128)(2,1)}, bf16[256,1792]{1,0:T(8,128)(2,1)}, u32[]{:S(2)}, u32[]{:S(2)}) collective-permute-start(bf16[256,1792]{1,0:T(8,128)(2,1)} %slice.129), channel_id=1, source_target_pairs={{0,4},{2,6},{4,0},{6,2},{1,5},{3,7},{5,1},{7,3},{8,12},{10,14},{12... | collective-permute-start | bytes 2752520 | tf_op jit(solution)/shard_map/ppermute | solution.py:20
  203.1 87.7 %reduce-scatter.3.cloned.1.call-start = ((), (), s32[]{:S(2)}) async-start(), calls=%async_computation.4 | async-start | bytes 2621440 | tf_op jit(solution)/shard_map/reduce_scatter | solution.py:220
  205.6 20.9 %collective-permute-start.4 = (bf16[256,1792]{1,0:T(8,128)(2,1)S(1)}, bf16[256,1792]{1,0:T(8,128)(2,1)S(1)}, u32[]{:S(2)}, u32[]{:S(2)}) collective-permute-start(bf16[256,1792]{1,0:T(8,128)(2,1)S(1)} %multiply_convert_fusion.8), channel_id=1, source_target_pairs={{0,1},{1,0},{2,3},{3,2},{4,5},{5,4},{6,7},{7,6},{8,9},{9,8},{10,11... | collective-permute-start | bytes 2752520 | tf_op jit(solution)/shard_map/ppermute | solution.py:20
  244.3 224.0 %all-reduce.2.cloned.1.call-start = ((), (), s32[]{:S(2)}) async-start(), calls=%async_computation.5 | async-start | bytes 4194304 | tf_op jit(solution)/shard_map/psum | solution.py:261
  294.4 5.5 collective-permute-start.7
  295.9 6.6 collective-permute-start.6
  296.1 6.5 collective-permute-start.5
  296.8 8.6 %collective-permute-start.15 = (bf16[256,256]{1,0:T(8,128)(2,1)S(1)}, bf16[256,256]{1,0:T(8,128)(2,1)S(1)}, u32[]{:S(2)}, u32[]{:S(2)}) collective-permute-start(bf16[256,256]{1,0:T(8,128)(2,1)S(1)} %bitcast.280), channel_id=1, source_target_pairs={{0,4},{2,6},{4,0},{6,2},{1,5},{3,7},{5,1},{7,3},{8,12},{10,14},{12... | collective-permute-start | bytes 393224 | tf_op jit(solution)/shard_map/ppermute | solution.py:224
  298.4 9.1 %collective-permute-start.14 = (bf16[256,256]{1,0:T(8,128)(2,1)S(1)}, bf16[256,256]{1,0:T(8,128)(2,1)S(1)}, u32[]{:S(2)}, u32[]{:S(2)}) collective-permute-start(bf16[256,256]{1,0:T(8,128)(2,1)S(1)} %bitcast.281), channel_id=1, source_target_pairs={{0,6},{2,4},{4,2},{6,0},{1,7},{3,5},{5,3},{7,1},{8,14},{10,12},{12... | collective-permute-start | bytes 393224 | tf_op jit(solution)/shard_map/ppermute | solution.py:224
  299.8 7.6 %collective-permute-start.13 = (bf16[256,256]{1,0:T(8,128)(2,1)S(1)}, bf16[256,256]{1,0:T(8,128)(2,1)S(1)}, u32[]{:S(2)}, u32[]{:S(2)}) collective-permute-start(bf16[256,256]{1,0:T(8,128)(2,1)S(1)} %bitcast.282), channel_id=1, source_target_pairs={{0,2},{2,0},{4,6},{6,4},{1,3},{3,1},{5,7},{7,5},{8,10},{10,8},{12,... | collective-permute-start | bytes 393224 | tf_op jit(solution)/shard_map/ppermute | solution.py:224
  305.3 8.5 %collective-permute-start.36 = (bf16[512,512]{1,0:T(8,128)(2,1)}, bf16[512,512]{1,0:T(8,128)(2,1)}, u32[]{:S(2)}, u32[]{:S(2)}) collective-permute-start(bf16[512,512]{1,0:T(8,128)(2,1)} %dynamic-slice_bitcast_fusion.4), channel_id=1, source_target_pairs={{0,2},{2,0},{4,6},{6,4},{1,3},{3,1},{5,7},{7,5},{8,10},{10,8},{12,... | collective-permute-start | bytes 1572872 | tf_op jit(solution)/shard_map/ppermute | solution.py:20
  310.3 6.0 collective-permute-start.26
  311.4 6.9 %collective-permute-start.16 = (bf16[512,512]{1,0:T(8,128)(2,1)}, bf16[512,512]{1,0:T(8,128)(2,1)}, u32[]{:S(2)}, u32[]{:S(2)}) collective-permute-start(bf16[512,512]{1,0:T(8,128)(2,1)} %dynamic-slice_bitcast_fusion.6), channel_id=1, source_target_pairs={{0,2},{2,0},{4,6},{6,4},{1,3},{3,1},{5,7},{7,5},{8,10},{10,8},{12,... | collective-permute-start | bytes 1572872 | tf_op jit(solution)/shard_map/ppermute | solution.py:20
  315.1 10.5 %collective-permute-start.37 = (bf16[256,512]{1,0:T(8,128)(2,1)S(1)}, bf16[256,512]{1,0:T(8,128)(2,1)S(1)}, u32[]{:S(2)}, u32[]{:S(2)}) collective-permute-start(bf16[256,512]{1,0:T(8,128)(2,1)S(1)} %dynamic-slice_bitcast_fusion.7), channel_id=1, source_target_pairs={{0,4},{2,6},{4,0},{6,2},{1,5},{3,7},{5,1},{7,3},{8,12},{10,14},{12... | collective-permute-start | bytes 786440 | tf_op jit(solution)/shard_map/ppermute | solution.py:20
  317.6 12.4 %collective-permute-start.27 = (bf16[256,512]{1,0:T(8,128)(2,1)S(1)}, bf16[256,512]{1,0:T(8,128)(2,1)S(1)}, u32[]{:S(2)}, u32[]{:S(2)}) collective-permute-start(bf16[256,512]{1,0:T(8,128)(2,1)S(1)} %dynamic-slice_bitcast_fusion.8), channel_id=1, source_target_pairs={{0,8},{8,0},{16,24},{24,16},{1,9},{9,1},{17,25},{25,17},{2,10},{10... | collective-permute-start | bytes 786440 | tf_op jit(solution)/shard_map/ppermute | solution.py:20
  319.5 12.4 %collective-permute-start.17 = (bf16[256,512]{1,0:T(8,128)(2,1)S(1)}, bf16[256,512]{1,0:T(8,128)(2,1)S(1)}, u32[]{:S(2)}, u32[]{:S(2)}) collective-permute-start(bf16[256,512]{1,0:T(8,128)(2,1)S(1)} %dynamic-slice_bitcast_fusion.9), channel_id=1, source_target_pairs={{0,1},{1,0},{2,3},{3,2},{4,5},{5,4},{6,7},{7,6},{8,9},{9,8},{10,11... | collective-permute-start | bytes 786440 | tf_op jit(solution)/shard_map/ppermute | solution.py:20
  325.6 7.0 %collective-permute-start.38 = (bf16[128,512]{1,0:T(8,128)(2,1)S(1)}, bf16[128,512]{1,0:T(8,128)(2,1)S(1)}, u32[]{:S(2)}, u32[]{:S(2)}) collective-permute-start(bf16[128,512]{1,0:T(8,128)(2,1)S(1)} %dynamic-slice_bitcast_fusion.10), channel_id=1, source_target_pairs={{0,1},{1,0},{2,3},{3,2},{4,5},{5,4},{6,7},{7,6},{8,9},{9,8},{10,11... | collective-permute-start | bytes 393224 | tf_op jit(solution)/shard_map/ppermute | solution.py:20
  330.0 11.4 %collective-permute-start.28 = (bf16[128,512]{1,0:T(8,128)(2,1)S(1)}, bf16[128,512]{1,0:T(8,128)(2,1)S(1)}, u32[]{:S(2)}, u32[]{:S(2)}) collective-permute-start(bf16[128,512]{1,0:T(8,128)(2,1)S(1)} %dynamic-slice_bitcast_fusion.11), channel_id=1, source_target_pairs={{0,16},{8,24},{16,0},{24,8},{1,17},{9,25},{17,1},{25,9},{2,18},{10... | collective-permute-start | bytes 393224 | tf_op jit(solution)/shard_map/ppermute | solution.py:20
  332.0 10.1 %collective-permute-start.18 = (bf16[128,512]{1,0:T(8,128)(2,1)S(1)}, bf16[128,512]{1,0:T(8,128)(2,1)S(1)}, u32[]{:S(2)}, u32[]{:S(2)}) collective-permute-start(bf16[128,512]{1,0:T(8,128)(2,1)S(1)} %dynamic-slice_bitcast_fusion.12), channel_id=1, source_target_pairs={{0,8},{8,0},{16,24},{24,16},{1,9},{9,1},{17,25},{25,17},{2,10},{10... | collective-permute-start | bytes 393224 | tf_op jit(solution)/shard_map/ppermute | solution.py:20
  332.7 11.4 %collective-permute-start.39 = (bf16[64,512]{1,0:T(8,128)(2,1)S(1)}, bf16[64,512]{1,0:T(8,128)(2,1)S(1)}, u32[]{:S(2)}, u32[]{:S(2)}) collective-permute-start(bf16[64,512]{1,0:T(8,128)(2,1)S(1)} %dynamic-slice_bitcast_fusion.13), channel_id=1, source_target_pairs={{0,8},{8,0},{16,24},{24,16},{1,9},{9,1},{17,25},{25,17},{2,10},{10... | collective-permute-start | bytes 196616 | tf_op jit(solution)/shard_map/ppermute | solution.py:20
  341.5 4.3 collective-permute-start.29
  342.3 6.5 collective-permute-start.19
  344.2 5.9 collective-permute-start.40
  345.9 4.5 collective-permute-start.30
  348.8 4.3 collective-permute-start.20
  350.1 4.9 collective-permute-start.41
  350.4 4.7 collective-permute-start.31
  353.2 4.0 collective-permute-start.21
  355.0 4.5 collective-permute-start.42
  355.1 5.8 collective-permute-start.32
  357.2 8.8 %collective-permute-start.22 = (bf16[64,512]{1,0:T(8,128)(2,1)S(1)}, bf16[64,512]{1,0:T(8,128)(2,1)S(1)}, u32[]{:S(2)}, u32[]{:S(2)}) collective-permute-start(bf16[64,512]{1,0:T(8,128)(2,1)S(1)} %pad_maximum_fusion.15), channel_id=1, source_target_pairs={{0,16},{8,24},{16,0},{24,8},{1,17},{9,25},{17,1},{25,9},{2,18},{10... | collective-permute-start | bytes 196616 | tf_op jit(solution)/shard_map/ppermute | solution.py:20
  359.6 6.6 collective-permute-start.43
  361.0 7.8 %collective-permute-start.33 = (bf16[128,512]{1,0:T(8,128)(2,1)S(1)}, bf16[128,512]{1,0:T(8,128)(2,1)S(1)}, u32[]{:S(2)}, u32[]{:S(2)}) collective-permute-start(bf16[128,512]{1,0:T(8,128)(2,1)S(1)} %pad_maximum_fusion.13), channel_id=1, source_target_pairs={{0,16},{8,24},{16,0},{24,8},{1,17},{9,25},{17,1},{25,9},{2,18},{10... | collective-permute-start | bytes 393224 | tf_op jit(solution)/shard_map/ppermute | solution.py:20
  366.1 6.4 collective-permute-start.23
  366.3 6.4 collective-permute-start.44
  368.8 7.3 %collective-permute-start.34 = (bf16[256,512]{1,0:T(8,128)(2,1)S(1)}, bf16[256,512]{1,0:T(8,128)(2,1)S(1)}, u32[]{:S(2)}, u32[]{:S(2)}) collective-permute-start(bf16[256,512]{1,0:T(8,128)(2,1)S(1)} %pad_maximum_fusion.10), channel_id=1, source_target_pairs={{0,8},{8,0},{16,24},{24,16},{1,9},{9,1},{17,25},{25,17},{2,10},{10... | collective-permute-start | bytes 786440 | tf_op jit(solution)/shard_map/ppermute | solution.py:20
  372.6 6.4 collective-permute-start.24
  372.9 6.4 collective-permute-start.45
  (23 other events, 118.4 us)
Sparse Core Ops, SparseCore 0:
  10.1 75.5 all-gather.2
  203.2 42.3 reduce-scatter.4
  247.9 42.8 reduce-scatter.2
  314.0 140.2 all-reduce.1
